TPU v7x, 256 devices: a whole 4x4x8 slice. The times are simulated.
256 devices in a mesh: sub: 32 (over x, z), site: 8 (over y, core).
Axes of the slice: x: 4, y: 4, z: 8, core: 2. Of those that a mesh axis runs over, the one named last changes fastest.
Arguments:
- sgt: bfloat16 [2048, 2, 2, 6, 128, 128], P('sub', None, None, None, 'site'), may hold values from -6 to 6
- mechanism: float32 [2048, 6], P('sub'), may hold values from -5 to 5
- slip: bfloat16 [2048, 64, 2, 128], P('sub'), may hold values from -0.109375 to 0.109375
- point_list: int32 [2048], replicated, may hold values from 0 to 2047, as said below
- subfault_counts: int32 [32], replicated, may hold values from 1 to 64, 1024 in all
Outputs:
- seismograms: bfloat16 [64, 2, 128, 2048], P('sub', None, 'site')
- psa: float32 [64, 2, 128, 40], P('sub', None, 'site')
Inputs may be any that keep to these rules, and one draw needn't show every extreme that they name: `point_list`: every SGT point is named by exactly one subfault slot. Of the 64 slots of each worker w (slots w * 64 to w * 64 + 63), exactly 2 name points of each reader block r (points r * 64 to r * 64 + 63). `subfault_counts`: the counts sum to 1024, and the largest is 64. Slots of a worker past its count are not part of the rupture.
All inputs are finite; a program needn't handle non-finite values.
Results may differ from a plain program's by a relative error of at most 0.0049.
Values may be sent and summed in bfloat16 or wider, within the bound.
A program may use at most 128 MiB of HBM per device.

v0:
```python
import math

import jax
import jax.numpy as jnp
from jax import lax
from jax.sharding import PartitionSpec as P

NT = 2048
PERIODS = 40


damping = 0.05
sample_step = 0.1


def synthesis_basis(freq_count, sample_count):
    freq_ids = jnp.arange(freq_count, dtype=jnp.int32)
    time_ids = jnp.arange(sample_count, dtype=jnp.int32)
    angles = (freq_ids[:, None] * time_ids[None, :] % sample_count).astype(jnp.float32) * (
        2.0 * math.pi / sample_count
    )
    norm_scale = 1.0 / math.sqrt(freq_count)
    return jnp.stack([norm_scale * jnp.cos(angles), -norm_scale * jnp.sin(angles)])


def oscillator_gains(period_count, freq_count, sample_count):
    period_ids = jnp.arange(period_count, dtype=jnp.float32)
    periods = 2.0 * jnp.exp(period_ids * (math.log(5.0) / max(period_count - 1, 1)))
    natural = 2.0 * math.pi / periods
    omega_bins = jnp.arange(freq_count, dtype=jnp.float32) * (
        2.0 * math.pi / (sample_count * sample_step)
    )
    squared_natural = (natural * natural)[:, None]
    real_part = squared_natural - (omega_bins * omega_bins)[None, :]
    imag_part = 2.0 * damping * natural[:, None] * omega_bins[None, :]
    magnitude = real_part * real_part + imag_part * imag_part
    return (-squared_natural * real_part / magnitude, squared_natural * imag_part / magnitude)


def rank_within_reader(readers, workers):
    onehot = (readers[:, :, None] == jnp.arange(workers, dtype=jnp.int32)[None, None, :]).astype(
        jnp.int32
    )
    return jnp.sum(onehot * jnp.cumsum(onehot, axis=1), axis=2) - 1


def project_strain(green_rows, moments):
    combined = moments[:, 0, None, None, None, None] * green_rows[:, :, :, 0].astype(jnp.float32)
    for strain in range(1, 6):
        combined = combined + moments[:, strain, None, None, None, None] * green_rows[
            :, :, :, strain
        ].astype(jnp.float32)
    return combined.astype(jnp.bfloat16)


def contract_slip(projected, slip_real, slip_imag):
    with_real = jnp.einsum(
        "jrcsf,jvf->rvcsf", projected, slip_real, preferred_element_type=jnp.float32
    )
    with_imag = jnp.einsum(
        "jrcsf,jvf->rvcsf", projected, slip_imag, preferred_element_type=jnp.float32
    )
    return jnp.stack([with_real[0] - with_imag[1], with_imag[0] + with_real[1]], axis=2)


def per_device(sgt, mechanism, slip, point_list, subfault_counts):
    workers = lax.axis_size("sub")
    worker = lax.axis_index("sub")
    slot_count = slip.shape[0]
    per_reader = sgt.shape[0]
    capacity = slot_count // workers
    freq_count = sgt.shape[-1]
    table_all = point_list.reshape(workers, slot_count)
    readers = table_all // per_reader
    local_rows = table_all % per_reader
    occurrence = rank_within_reader(readers, workers)
    rank_ids = jnp.arange(capacity, dtype=jnp.int32)
    held_here = readers == worker
    chosen = (held_here[:, None, :] & (occurrence[:, None, :] == rank_ids[None, :, None])).astype(
        jnp.int32
    )
    send_rows = jnp.sum(chosen * local_rows[:, None, :], axis=2).reshape(-1)
    own_readers = lax.dynamic_index_in_dim(readers, worker, 0, keepdims=False)
    own_occ = lax.dynamic_index_in_dim(occurrence, worker, 0, keepdims=False)
    reader_ids = jnp.arange(workers, dtype=jnp.int32)
    matched = (
        (own_readers[None, None, :] == reader_ids[:, None, None])
        & (own_occ[None, None, :] == rank_ids[None, :, None])
    ).astype(jnp.int32)
    slot_order = jnp.sum(
        matched * jnp.arange(slot_count, dtype=jnp.int32)[None, None, :], axis=2
    ).reshape(-1)
    own_count = lax.dynamic_index_in_dim(subfault_counts, worker, 0, keepdims=False)
    live_mask = (jnp.arange(slot_count, dtype=jnp.int32) < own_count).astype(slip.dtype)
    slip_live = slip * live_mask[:, None, None, None]
    slip_arranged = jnp.take(slip_live, slot_order, axis=0)
    slip_real = slip_arranged[:, :, 0]
    slip_imag = slip_arranged[:, :, 1]
    moments_arranged = jnp.take(mechanism, slot_order, axis=0)
    outgoing = jnp.take(sgt, send_rows, axis=0)
    partial_value = contract_slip(
        project_strain(
            lax.all_to_all(outgoing, "sub", split_axis=0, concat_axis=0, tiled=True),
            moments_arranged,
        ),
        slip_real,
        slip_imag,
    )
    basis = synthesis_basis(freq_count, NT)
    spectrum = lax.psum_scatter(partial_value, "sub", scatter_dimension=0, tiled=True)
    motion = jnp.einsum("vcrsf,rft->vcst", spectrum, basis, precision=lax.Precision.HIGHEST)
    gain_real, gain_imag = oscillator_gains(PERIODS, freq_count, NT)
    spec_real = spectrum[:, :, 0]
    spec_imag = spectrum[:, :, 1]
    gain_re = gain_real[:, None, None, None, :]
    gain_im = gain_imag[:, None, None, None, :]
    resp_real = gain_re * spec_real[None] - gain_im * spec_imag[None]
    resp_imag = gain_re * spec_imag[None] + gain_im * spec_real[None]
    response = jnp.stack([resp_real, resp_imag], axis=3).astype(jnp.bfloat16)
    basis_low = basis.astype(jnp.bfloat16)
    response_wave = jnp.einsum(
        "kvcrsf,rft->kvcst", response, basis_low, preferred_element_type=jnp.float32
    )
    peak_values = jnp.max(jnp.abs(response_wave), axis=4)
    return (motion.astype(jnp.bfloat16), jnp.transpose(peak_values, (1, 2, 3, 0)))


def solution(mesh):
    in_specs = (
        P("sub", None, None, None, "site", None),
        P("sub", None),
        P("sub", None, None, None),
        P(),
        P(),
    )
    out_specs = (P("sub", None, "site", None), P("sub", None, "site", None))
    return jax.shard_map(
        per_device, mesh=mesh, in_specs=in_specs, out_specs=out_specs, check_vma=False
    )
```

profile of v0, /device:TPU:1, one launch (start us, length us, event | category | flops | bytes accessed | tf_op | source)
XLA Modules:
  0.0 428.4 jit_solution(16556636915324530266)
XLA Ops:
  7.2 0.8 reshape.513
  8.0 1.7 select_reduce_fusion
  10.3 6.8 %gather_fusion.2 = bf16[64,2,2,6,16,128]{5,4,3,2,1,0:T(8,128)(2,1)} fusion(bf16[64,2,2,6,16,128]{5,4,3,2,1,0:T(8,128)(2,1)} %param.5, s32[1024]{0:T(1024)S(1)} %pad_clamp_fusion), kind=kCustom, calls=%fused_computation.2 | custom fusion | bytes 12583168 | tf_op jit(solution)/shard_map/jit(_take)/gather | solution.py:100
  17.1 6.1 %broadcast_select_fusion = bf16[64,2,2,6,16,128]{5,4,3,2,1,0:T(8,128)(2,1)} fusion(bf16[64,2,2,6,16,128]{5,4,3,2,1,0:T(8,128)(2,1)} %gather_fusion.2, pred[64]{0:T(512)(128)(4,1)S(1)} %compare_and_fusion), kind=kLoop, calls=%fused_computation.5 | loop fusion | flops 3145728 | bytes 12582976 | tf_op jit(solution)/shard_map/jit(_take)/select_n | solution.py:100
  23.2 12.1 %all-to-all-start = ((bf16[64,2,2,6,16,128]{5,4,3,2,1,0:T(8,128)(2,1)}), bf16[64,2,2,6,16,128]{5,4,3,2,1,0:T(8,128)(2,1)}, u32[]{:S(2)}, u32[]{:S(2)}) async-start(bf16[64,2,2,6,16,128]{5,4,3,2,1,0:T(8,128)(2,1)} %broadcast_select_fusion), calls=%async_computation | async-start | bytes 12582912 | tf_op jit(solution)/shard_map/all_to_all | solution.py:103
  37.4 0.6 compare_convert_fusion
  38.0 1.7 copy_multiply_fusion
  39.7 2.5 gather_fusion
  42.2 6.4 %copy.110 = bf16[64,64,2,128]{1,0,3,2:T(8,128)(2,1)} copy(bf16[64,64,2,128]{3,1,2,0:T(8,128)(2,1)S(1)} %gather_fusion) | data formatting | bytes 4194304 | tf_op jit(solution)/shard_map/jit(_take)/gather | solution.py:96
  49.0 4.6 %broadcast_select_fusion.1 = bf16[64,64,2,128]{1,0,3,2:T(8,128)(2,1)} fusion(bf16[64,64,2,128]{1,0,3,2:T(8,128)(2,1)} %copy.110, pred[64]{0:T(512)(128)(4,1)S(1)} %compare_and_fusion.1), kind=kLoop, calls=%fused_computation.7 | loop fusion | flops 1048576 | bytes 4194368 | tf_op jit(solution)/shard_map/jit(_take)/select_n | solution.py:96
  53.6 119.8 %all-to-all-done = bf16[64,2,2,6,16,128]{5,4,3,2,1,0:T(8,128)(2,1)} async-done(((bf16[64,2,2,6,16,128]{5,4,3,2,1,0:T(8,128)(2,1)}), bf16[64,2,2,6,16,128]{5,4,3,2,1,0:T(8,128)(2,1)}, u32[]{:S(2)}, u32[]{:S(2)}) %all-to-all-start) | async-done | bytes 6291488 | tf_op jit(solution)/shard_map/all_to_all | solution.py:103
  173.5 3.7 fusion.6
  177.2 4.4 %copy.128 = bf16[64,2,2,16,128]{0,3,2,4,1:T(8,128)(2,1)} copy(bf16[64,2,2,16,128]{4,3,2,1,0:T(8,128)(2,1)S(1)} %fusion.6) | data formatting | bytes 2097152 | tf_op jit(solution)/shard_map/convert_element_type | solution.py:53
  181.5 3.5 copy.119
  185.0 3.1 convolution_bitcast_fusion.1
  188.5 0.7 convolution_bitcast_fusion.2
  190.1 2.5 pad_maximum_fusion
  192.6 4.9 %copy.124 = f32[64,2,2,16,128]{4,3,2,1,0:T(8,128)} copy(f32[64,2,2,16,128]{0,3,1,4,2:T(8,128)} %pad_maximum_fusion) | data formatting | bytes 4194304 | tf_op jit(solution)/shard_map/stack | solution.py:63
  197.7 4.1 sine_multiply_fusion
  201.9 212.4 %reduce-scatter.2.cloned.1.call-done = f32[2,2,2,16,128]{4,3,2,1,0:T(8,128)} async-done(((f32[64,2,2,16,128]{4,3,2,1,0:T(8,128)}), f32[2,2,2,16,128]{4,3,2,1,0:T(8,128)}) %reduce-scatter.2.cloned.1.call-update) | async-done | bytes 65552 | tf_op jit(solution)/shard_map/reduce_scatter | solution.py:110
  414.3 0.8 slice_bitcast_fusion.13
  415.5 3.3 fusion
  418.8 0.7 copy.125
  419.5 2.1 fusion.1
  (46 shorter events, 4.8 us)
Async XLA Ops:
  23.2 12.8 %copy-start.3 = (f32[64,6]{0,1:T(8,128)S(1)}, f32[64,6]{0,1:T(8,128)}, u32[]{:S(2)}) copy-start(f32[64,6]{0,1:T(8,128)} %param.6) | copy-start | bytes 4612
  23.2 12.9 %copy-start.4 = (s32[32]{0:T(128)S(1)}, s32[32]{0:T(128)}, u32[]{:S(2)}) copy-start(s32[32]{0:T(128)} %param.9) | copy-start | bytes 388
  23.2 14.8 %copy-start.1 = (bf16[64,64,2,128]{3,2,1,0:T(2,128)(2,1)S(1)}, bf16[64,64,2,128]{3,2,1,0:T(2,128)(2,1)}, u32[]{:S(2)}) copy-start(bf16[64,64,2,128]{3,2,1,0:T(2,128)(2,1)} %param.7) | copy-start | bytes 6291460
  23.2 150.2 %all-to-all-start = ((bf16[64,2,2,6,16,128]{5,4,3,2,1,0:T(8,128)(2,1)}), bf16[64,2,2,6,16,128]{5,4,3,2,1,0:T(8,128)(2,1)}, u32[]{:S(2)}, u32[]{:S(2)}) async-start(bf16[64,2,2,6,16,128]{5,4,3,2,1,0:T(8,128)(2,1)} %broadcast_select_fusion), calls=%async_computation | async-start | bytes 12582912 | tf_op jit(solution)/shard_map/all_to_all | solution.py:103
  35.3 379.0 %reduce-scatter.2.cloned.1.call-start = ((), (), s32[]{:S(2)}) async-start(), calls=%async_computation.2 | async-start | bytes 2162688 | tf_op jit(solution)/shard_map/reduce_scatter | solution.py:110
  185.0 3.5 copy-start
  415.5 4.0 copy-start.2
Sparse Core Ops, SparseCore 0:
  197.7 216.5 reduce-scatter.1
where the time goes:
time: 433 us; the launch traced here: 428 us
  waiting for transfers between devices  332 us (77%)
  local copies, waits for them, and re-layouts  33.5 us (8%)
  other arithmetic  26.9 us (6%)
  between operations  14.3 us (3%)
  starting transfers between devices  12.3 us (3%)
  matrix products  9.11 us (2%)
    reduce_scatter x1, waiting for transfers between devices, per_device(): lax.psum_scatter(partial_value, 'sub', scatter_dimension=0, tiled=True)  212 us
    all_to_all x1, waiting for transfers between devices, per_device(): lax.all_to_all(outgoing, 'sub', split_axis=0, concat_axis=0, tiled=True)  120 us
    all_to_all x1, starting transfers between devices, per_device(): lax.all_to_all(outgoing, 'sub', split_axis=0, concat_axis=0, tiled=True)  12.1 us
    gather x2, local copies, waits for them, and re-layouts, per_device(): slip_arranged = jnp.take(slip_live, slot_order, axis=0)  8.97 us
  transfers between devices with their start and end apart: 2, of which 2 were waited for; matrix products, arithmetic and copies ran while one was open for 5% of the time, Pallas kernels for 0%

commit v1 on v0

v1 whole, which is shorter than its diff:
```python
import functools
import math

import jax
import jax.numpy as jnp
import numpy as np
from jax import lax
from jax.experimental import pallas as pl
from jax.experimental.pallas import tpu as pltpu
from jax.sharding import PartitionSpec as P

NT = 2048
PERIODS = 40
CHUNKS = 2
MESH = pl.DeviceIdType.MESH

damping = 0.05
sample_step = 0.1


def bins_in_order(freq_count):
    kappa = np.arange(freq_count)
    quarter = freq_count // 4
    return 4 * (kappa % quarter) + kappa // quarter


def synthesis_basis(freq_count, sample_count):
    freq_ids = bins_in_order(freq_count)
    angles = (freq_ids[:, None] * np.arange(sample_count)[None, :] % sample_count) * (2.0 * math.pi / sample_count)
    scale = 1.0 / math.sqrt(freq_count)
    both = np.concatenate([scale * np.cos(angles), -scale * np.sin(angles)], axis=0).astype(np.float32)
    high = both.astype(jnp.bfloat16)
    low = (both - high.astype(np.float32)).astype(jnp.bfloat16)
    return high, low


def oscillator_gains(period_count, freq_count, sample_count):
    periods = 2.0 * np.exp(np.arange(period_count) * (math.log(5.0) / max(period_count - 1, 1)))
    natural = 2.0 * math.pi / periods
    omega = bins_in_order(freq_count) * (2.0 * math.pi / (sample_count * sample_step))
    squared = (natural * natural)[:, None]
    real_part = squared - (omega * omega)[None, :]
    imag_part = 2.0 * damping * natural[:, None] * omega[None, :]
    magnitude = real_part * real_part + imag_part * imag_part
    return np.stack([-squared * real_part / magnitude, squared * imag_part / magnitude]).astype(np.float32)


def spectrum_kernel(
    dims, points_ref, counts_ref, mech_ref, slip_hbm, sgt_hbm, spec_ref,
    table, table_smem, sgt, slip, mech_out, mech_in, wide, slip_out, slip_in, flip, proj_out, proj_in,
    pieces, piece_flip, part, part_out, part_in,
    table_sem, sgt_sem, slip_sem, mech_ssem, mech_rsem, slip_ssem, slip_rsem, proj_ssem, proj_rsem,
    ring_ssem, ring_rsem, pair_ssem, pair_rsem, part_ssem, part_rsem,
):
    nx, nz, ny = dims
    workers = nx * nz
    slots, vq, freqs = slip.shape
    rows_pc = 2 * 2 * sgt.shape[4]
    per_reader = sgt.shape[0]
    share = freqs // nx
    group = workers // CHUNKS
    packs = points_ref.shape[1] // slots
    table_rows = points_ref.shape[0]
    lanes = points_ref.shape[1]

    me = lax.axis_index("sub")
    site = lax.axis_index("site")
    my_x = me // nz
    my_y = site // 2
    core = site % 2

    get_slip = pltpu.make_async_copy(slip_hbm, slip, slip_sem)
    get_slip.start()
    get_sgt = pltpu.make_async_copy(sgt_hbm, sgt, sgt_sem)
    get_sgt.start()

    def peer_of(step):
        return lax.rem(me + step, workers)

    def site_of(step):
        return lax.rem(my_y + step, ny) * 2 + core

    other = my_y * 2 + (1 - core)

    barrier = pltpu.get_barrier_semaphore()

    @pl.loop(1, workers)
    def _(step):
        pl.semaphore_signal(barrier, inc=1, device_id={"sub": peer_of(step)}, device_id_type=MESH)

    for step in range(1, ny):
        pl.semaphore_signal(barrier, inc=1, device_id={"site": site_of(step)}, device_id_type=MESH)
    pl.semaphore_signal(barrier, inc=1, device_id={"site": other}, device_id_type=MESH)

    points = points_ref[...]
    lane = lax.broadcasted_iota(jnp.int32, (table_rows, lanes), 1)
    out_lane = lax.broadcasted_iota(jnp.int32, (table_rows, 128), 1)
    mine = points // per_reader == me
    local = points % per_reader
    named = jnp.zeros((table_rows, 128), jnp.int32)
    for pack in range(packs):
        here = mine & (lane // slots == pack)
        first = jnp.min(jnp.where(here, lane, lanes), axis=1, keepdims=True)
        last = jnp.max(jnp.where(here, lane, -1), axis=1, keepdims=True)
        for k, found in enumerate((first, last)):
            row = jnp.sum(jnp.where(here & (lane == found), local, 0), axis=1, keepdims=True)
            named = jnp.where(out_lane == pack * 2 + k, row, named)
    table[pl.ds(0, table_rows), :] = named

    my_points = points_ref[pl.ds(me // packs, 1), :]
    lane = lax.broadcasted_iota(jnp.int32, (workers, lanes), 1)
    out_lane = lax.broadcasted_iota(jnp.int32, (workers, 128), 1)
    reader = lax.broadcasted_iota(jnp.int32, (workers, lanes), 0)
    base = lax.rem(me, packs) * slots
    here = (my_points // per_reader == reader) & (lane >= base) & (lane < base + slots)
    first = jnp.min(jnp.where(here, lane, lanes), axis=1, keepdims=True)
    last = jnp.max(jnp.where(here, lane, -1), axis=1, keepdims=True)
    table[pl.ds(table_rows, workers), :] = jnp.clip(jnp.where(out_lane == 0, first, last) - base, 0, slots - 1)
    to_smem = pltpu.make_async_copy(table, table_smem, table_sem)
    to_smem.start()

    live = lane - base < counts_ref[me]
    moments = jnp.concatenate([mech_ref[...]] * packs, axis=1)
    sent = jnp.zeros((workers, 128), jnp.float32)
    for k, found in enumerate((first, last)):
        chosen = here & live & (lane == found)
        for m in range(6):
            value = jnp.sum(jnp.where(chosen, moments[m : m + 1, :], 0.0), axis=1, keepdims=True)
            sent = jnp.where(out_lane == k * 6 + m, value, sent)
    mech_out[...] = sent.reshape(workers, 1, 128)

    to_smem.wait()
    get_slip.wait()
    my_k = site // nx
    x_of_piece = lax.rem(site, nx)

    @pl.loop(0, nz)
    def _(zr):
        slot = table_smem[table_rows + x_of_piece * nz + zr, my_k]
        turned = slip[slot].astype(jnp.float32).T.astype(jnp.bfloat16)
        for x in range(nx):
            slip_out[x * nz + zr] = turned[x * share : (x + 1) * share]

    pl.semaphore_wait(barrier, workers - 1 + ny)

    def mech_copy(peer):
        return pltpu.make_async_remote_copy(
            src_ref=mech_out.at[peer], dst_ref=mech_in.at[me], send_sem=mech_ssem, recv_sem=mech_rsem,
            device_id={"sub": peer}, device_id_type=MESH,
        )

    chunk_of_me = me // group

    def slip_copy(peer):
        return pltpu.make_async_remote_copy(
            src_ref=slip_out.at[peer], dst_ref=slip_in.at[me], send_sem=slip_ssem,
            recv_sem=slip_rsem.at[chunk_of_me], device_id={"sub": peer}, device_id_type=MESH,
        )

    @pl.loop(1, workers)
    def _(step):
        mech_copy(peer_of(step)).start()

    pltpu.make_async_copy(mech_out.at[me], mech_in.at[me], mech_rsem).start()

    @pl.loop(1, workers)
    def _(step):
        slip_copy(peer_of(step)).start()

    pltpu.make_async_copy(slip_out.at[me], slip_in.at[me], slip_rsem.at[chunk_of_me]).start()

    def wait_bytes(ref, sem):
        pltpu.make_async_copy(ref, ref, sem).wait()

    get_sgt.wait()
    wait_bytes(mech_in, mech_rsem)
    gathered = mech_in[...].reshape(workers, 128)
    for column in range(12):
        wide[column] = jnp.broadcast_to(gathered[:, column : column + 1], (workers, freqs))

    sites = sgt.shape[4]

    def project(chunk):
        @pl.loop(0, group)
        def _(index):
            worker = chunk * group + index
            blocks = []
            for k in range(2):
                point = table_smem[worker // packs, lax.rem(worker, packs) * 2 + k]
                weights = [
                    jnp.broadcast_to(wide[k * 6 + m, pl.ds(worker, 1), :], (sites, freqs)) for m in range(6)
                ]
                for part_id in range(2):
                    for c in range(2):
                        total = weights[0] * sgt[point, part_id, c, 0].astype(jnp.float32)
                        for m in range(1, 6):
                            total = total + weights[m] * sgt[point, part_id, c, m].astype(jnp.float32)
                        blocks.append(total)
            turned = jnp.concatenate(blocks, axis=0).T
            flip[pl.ds(index, freqs, stride=group), :] = turned

        for x in range(nx):
            rows = share * group
            block = flip[pl.ds(x * rows, rows), :].astype(jnp.bfloat16)
            proj_out[chunk, x] = block.reshape(share, group, 2 * rows_pc)
        for step in range(1, nx):
            proj_copy(chunk, step).start()
        pltpu.make_async_copy(proj_out.at[chunk, my_x], proj_in.at[chunk, my_x], proj_rsem.at[chunk]).start()

    my_z = lax.rem(me, nz)

    def proj_copy(chunk, step):
        x = lax.rem(my_x + step, nx)
        return pltpu.make_async_remote_copy(
            src_ref=proj_out.at[chunk, x], dst_ref=proj_in.at[chunk, my_x], send_sem=proj_ssem.at[chunk],
            recv_sem=proj_rsem.at[chunk], device_id={"sub": x * nz + my_z}, device_id_type=MESH,
        )

    def ring_copy(chunk, step):
        piece = pieces.at[chunk, site]
        return pltpu.make_async_remote_copy(
            src_ref=piece, dst_ref=piece, send_sem=ring_ssem.at[chunk, step - 1],
            recv_sem=ring_rsem.at[chunk, step - 1], device_id={"site": site_of(step)}, device_id_type=MESH,
        )

    def pair_copy(chunk, y):
        piece = pieces.at[chunk, y * 2 + core]
        return pltpu.make_async_remote_copy(
            src_ref=piece, dst_ref=piece, send_sem=pair_ssem.at[chunk], recv_sem=pair_rsem.at[chunk],
            device_id={"site": other}, device_id_type=MESH,
        )

    def share_slip(chunk):
        wait_bytes(slip_in.at[pl.ds(chunk * group, group)], slip_rsem.at[chunk])
        for index in range(group):
            piece_flip[pl.ds(index, share, stride=group), :] = slip_in[chunk * group + index].astype(jnp.float32)
        pieces[chunk, site] = piece_flip[...].astype(jnp.bfloat16).reshape(share, group, vq)
        for step in range(1, ny):
            ring_copy(chunk, step).start()
        pair_copy(chunk, my_y).start()

    for chunk in range(CHUNKS):
        project(chunk)
        share_slip(chunk)
    for chunk in range(CHUNKS):
        for step in range(1, ny):
            y = lax.rem(my_y + ny - step, ny)
            wait_bytes(pieces.at[chunk, y * 2 + core], ring_rsem.at[chunk, step - 1])
            pair_copy(chunk, y).start()
    for chunk in range(CHUNKS):
        wait_bytes(proj_in.at[chunk], proj_rsem.at[chunk])
        wait_bytes(pieces.at[chunk, pl.ds(0, ny)], pair_rsem.at[chunk])

    quads = share // 4
    lane = lax.broadcasted_iota(jnp.int32, (rows_pc // 2, vq), 1)
    even = lane % 2 == 0

    @pl.loop(0, quads)
    def _(quad):
        blocks = []
        for inner in range(4):
            f = quad * 4 + inner
            projected = jnp.concatenate(
                [proj_in[chunk, x, f] for chunk in range(CHUNKS) for x in range(nx)], axis=0
            ).T
            left = jnp.concatenate([projected[:rows_pc], projected[rows_pc:]], axis=1)
            right = jnp.concatenate(
                [pieces[chunk, k * nx + x, f] for k in range(2) for chunk in range(CHUNKS) for x in range(nx)], axis=0
            )
            both = jnp.dot(left, right, preferred_element_type=jnp.float32)
            straight, crossed = both[: rows_pc // 2], both[rows_pc // 2 :]
            swapped = jnp.where(even, -pltpu.roll(crossed, vq - 1, 1), pltpu.roll(crossed, 1, 1))
            blocks.append(straight + swapped)
        part[pl.ds(quad, vq, stride=quads), :] = jnp.concatenate(blocks, axis=0).T

    width = 4 * quads
    part_out[...] = part[...].astype(jnp.bfloat16).reshape(workers, width, 128)

    def part_copy(peer):
        return pltpu.make_async_remote_copy(
            src_ref=part_out.at[peer], dst_ref=part_in.at[me], send_sem=part_ssem, recv_sem=part_rsem,
            device_id={"sub": peer}, device_id_type=MESH,
        )

    @pl.loop(1, workers)
    def _(step):
        part_copy(peer_of(step)).start()

    pltpu.make_async_copy(part_out.at[me], part_in.at[me], part_rsem).start()

    wait_bytes(mech_out.at[pl.ds(0, workers - 1)], mech_ssem)
    wait_bytes(slip_out.at[pl.ds(0, workers - 1)], slip_ssem)
    for chunk in range(CHUNKS):
        wait_bytes(proj_out.at[chunk, pl.ds(0, nx - 1)], proj_ssem.at[chunk])
        for step in range(1, ny):
            wait_bytes(pieces.at[chunk, site], ring_ssem.at[chunk, step - 1])
        wait_bytes(pieces.at[chunk, pl.ds(0, ny)], pair_ssem.at[chunk])
    wait_bytes(part_in, part_rsem)
    wait_bytes(part_out.at[pl.ds(0, workers - 1)], part_ssem)

    totals = []
    for x in range(nx):
        total = part_in[x * nz].astype(jnp.float32)
        for z in range(1, nz):
            total = total + part_in[x * nz + z].astype(jnp.float32)
        totals.append(total)
    for e in range(2):
        for q in range(2):
            start = (e * 2 + q) * quads
            turned = jnp.concatenate([total[start : start + quads] for total in totals], axis=0).T
            rows = rows_pc // 2
            spec_ref[e, q] = jnp.concatenate([turned[i * rows : (i + 1) * rows] for i in range(4)], axis=1)


def spectrum_call(dims, sgt, mechanism, slip, point_list, subfault_counts):
    nx, nz, ny = dims
    workers = nx * nz
    slots, variations, _, freqs = slip.shape
    vq = variations * 2
    rows_pc = 4 * sgt.shape[4]
    share = freqs // nx
    group = workers // CHUNKS
    packs = max(1, min(128 // slots, 2))
    table_rows = workers // packs
    points = point_list.reshape(table_rows, packs * slots)
    width = share
    bf16, f32 = jnp.bfloat16, jnp.float32
    dma = pltpu.SemaphoreType.DMA
    vmem, smem, anywhere = (pl.BlockSpec(memory_space=s) for s in (pltpu.VMEM, pltpu.SMEM, pl.ANY))
    return pl.pallas_call(
        functools.partial(spectrum_kernel, dims),
        out_shape=jax.ShapeDtypeStruct((2, 2, rows_pc // 2, freqs), f32),
        in_specs=[vmem, smem, vmem, anywhere, anywhere],
        out_specs=vmem,
        scratch_shapes=[
            pltpu.VMEM((table_rows + workers, 128), jnp.int32),
            pltpu.SMEM((table_rows + workers, 128), jnp.int32),
            pltpu.VMEM(sgt.shape, bf16),
            pltpu.VMEM((slots, vq, freqs), bf16),
            pltpu.VMEM((workers, 1, 128), f32),
            pltpu.VMEM((workers, 1, 128), f32),
            pltpu.VMEM((12, workers, freqs), f32),
            pltpu.VMEM((workers, share, vq), bf16),
            pltpu.VMEM((workers, share, vq), bf16),
            pltpu.VMEM((freqs * group, 2 * rows_pc), f32),
            pltpu.VMEM((CHUNKS, nx, share, group, 2 * rows_pc), bf16),
            pltpu.VMEM((CHUNKS, nx, share, group, 2 * rows_pc), bf16),
            pltpu.VMEM((CHUNKS, ny * 2, share, group, vq), bf16),
            pltpu.VMEM((share * group, vq), f32),
            pltpu.VMEM((workers * width, 128), f32),
            pltpu.VMEM((workers, width, 128), bf16),
            pltpu.VMEM((workers, width, 128), bf16),
            dma, dma, dma, dma, dma, dma, dma((CHUNKS,)), dma((CHUNKS,)), dma((CHUNKS,)),
            dma((CHUNKS, ny - 1)), dma((CHUNKS, ny - 1)), dma((CHUNKS,)), dma((CHUNKS,)), dma, dma,
        ],
        compiler_params=pltpu.CompilerParams(
            collective_id=0, has_side_effects=True, vmem_limit_bytes=63 * 1024 * 1024
        ),
        name="spectrum",
    )(points, subfault_counts, mechanism.T, slip.reshape(slots, vq, freqs), sgt)


def synthesis_kernel(spec_ref, gain_ref, high_ref, low_ref, seis_ref, psa_ref, response, source, peak):
    step = pl.program_id(0)
    periods = gain_ref.shape[1]
    freqs = gain_ref.shape[2]
    rows = source.shape[1]

    @pl.when(step == 0)
    def _():
        real = jnp.concatenate([spec_ref[0, 0], spec_ref[1, 0]], axis=0)
        imag = jnp.concatenate([spec_ref[0, 1], spec_ref[1, 1]], axis=0)
        spectrum = jnp.concatenate([real, imag], axis=1)
        top = spectrum.astype(jnp.bfloat16)
        source[0] = top
        source[1] = (spectrum - top.astype(jnp.float32)).astype(jnp.bfloat16)
        for q in range(periods):
            g0 = gain_ref[0, q : q + 1, :]
            g1 = gain_ref[1, q : q + 1, :]
            response[pl.ds(q * rows, rows), pl.ds(0, freqs)] = (g0 * real - g1 * imag).astype(jnp.bfloat16)
            response[pl.ds(q * rows, rows), pl.ds(freqs, freqs)] = (g0 * imag + g1 * real).astype(jnp.bfloat16)
        peak[...] = jnp.zeros_like(peak)

    high = high_ref[...]
    motion = (
        jnp.dot(source[0], high, preferred_element_type=jnp.float32)
        + jnp.dot(source[1], high, preferred_element_type=jnp.float32)
        + jnp.dot(source[0], low_ref[...], preferred_element_type=jnp.float32)
    )
    seis_ref[...] = motion.astype(jnp.bfloat16)
    per = 8
    for start in range(0, periods, per):
        part = pl.ds(start * rows, per * rows)
        wave = jnp.abs(jnp.dot(response[part, :], high, preferred_element_type=jnp.float32))
        most = peak[part, :]
        for t in range(0, wave.shape[1], 128):
            most = jnp.maximum(most, wave[:, t : t + 128])
        peak[part, :] = most

    @pl.when(step == pl.num_programs(0) - 1)
    def _():
        lane = lax.broadcasted_iota(jnp.int32, (rows, periods), 1)
        total = jnp.zeros((rows, periods), jnp.float32)
        for q in range(periods):
            most = jnp.max(peak[pl.ds(q * rows, rows), :], axis=1, keepdims=True)
            total = jnp.where(lane == q, most, total)
        psa_ref[...] = total


def synthesis_call(spec):
    rows, freqs = 2 * spec.shape[2], spec.shape[3]
    high, low = synthesis_basis(freqs, NT)
    gains = oscillator_gains(PERIODS, freqs, NT)
    tile = 256
    return pl.pallas_call(
        synthesis_kernel,
        grid=(NT // tile,),
        out_shape=(
            jax.ShapeDtypeStruct((rows, NT), jnp.bfloat16),
            jax.ShapeDtypeStruct((rows, PERIODS), jnp.float32),
        ),
        in_specs=[
            pl.BlockSpec(spec.shape, lambda t: (0, 0, 0, 0)),
            pl.BlockSpec(gains.shape, lambda t: (0, 0, 0)),
            pl.BlockSpec((2 * freqs, tile), lambda t: (0, t)),
            pl.BlockSpec((2 * freqs, tile), lambda t: (0, t)),
        ],
        out_specs=(
            pl.BlockSpec((rows, tile), lambda t: (0, t)),
            pl.BlockSpec((rows, PERIODS), lambda t: (0, 0)),
        ),
        scratch_shapes=[
            pltpu.VMEM((PERIODS * rows, 2 * freqs), jnp.bfloat16),
            pltpu.VMEM((2, rows, 2 * freqs), jnp.bfloat16),
            pltpu.VMEM((PERIODS * rows, 128), jnp.float32),
        ],
        compiler_params=pltpu.CompilerParams(dimension_semantics=("arbitrary",)),
        name="synthesis",
    )(spec, jnp.asarray(gains), jnp.asarray(high), jnp.asarray(low))


def per_device(dims, sgt, mechanism, slip, point_list, subfault_counts):
    spec = spectrum_call(dims, sgt, mechanism, slip, point_list, subfault_counts)
    seis, psa = synthesis_call(spec)
    sites = sgt.shape[4]
    return seis.reshape(2, 2, sites, NT), psa.reshape(2, 2, sites, PERIODS)


def solution(mesh):
    workers, site_devices = mesh.shape["sub"], mesh.shape["site"]
    nx = site_devices // 2
    dims = (nx, workers // nx, site_devices // 2)
    in_specs = (
        P("sub", None, None, None, "site", None),
        P("sub", None),
        P("sub", None, None, None),
        P(),
        P(),
    )
    out_specs = (P("sub", None, "site", None), P("sub", None, "site", None))
    return jax.shard_map(
        functools.partial(per_device, dims), mesh=mesh, in_specs=in_specs, out_specs=out_specs, check_vma=False
    )
```

time: 433 us -> 57.9 us (0.13); the launches traced: 428 us -> 57.7 us
  waiting for transfers between devices: 332 us -> 0 us
  Pallas kernels: 0 us -> 57 us
  local copies, waits for them, and re-layouts: 33.5 us -> 0 us
  other arithmetic: 26.9 us -> 0 us
  between operations: 14.3 us -> 0.64 us
  starting transfers between devices: 12.3 us -> 0 us
  matrix products: 9.11 us -> 0 us
    reduce_scatter x1 -> x0, waiting for transfers between devices: 212 us -> none  [per_device(): lax.psum_scatter(partial_value, 'sub', scatter_dimension=0, tiled=True)]
    all_to_all x1 -> x0, waiting for transfers between devices: 120 us -> none  [per_device(): lax.all_to_all(outgoing, 'sub', split_axis=0, concat_axis=0, tiled=True)]
    pallas_call x0 -> x2, Pallas kernels: none -> 57 us  [the longest x1 48.5 us: spectrum_call(): pl.pallas_call(functools.partial(spectrum_kernel, dims), out_shape=jax.Sh...]
    gather x4 -> x0, local copies, waits for them, and re-layouts: 16.4 us -> none  [the longest x2 8.97 us: per_device(): slip_arranged = jnp.take(slip_live, slot_order, axis=0)]
    all_to_all x1 -> x0, starting transfers between devices: 12.1 us -> none  [per_device(): lax.all_to_all(outgoing, 'sub', split_axis=0, concat_axis=0, tiled=True)]
    select_n x6 -> x0, other arithmetic: 10.8 us -> none  [the longest x2 6.11 us: per_device(): outgoing = jnp.take(sgt, send_rows, axis=0)]
    dot_general x4 -> x0, matrix products: 9.11 us -> none  [the longest x1 3.28 us: per_device(): jnp.einsum('kvcrsf,rft->kvcst', response, basis_low, preferred_element_ty...]
    convert_element_type x2 -> x0, local copies, waits for them, and re-layouts: 7.85 us -> none  [project_strain(): return combined.astype(jnp.bfloat16)]
  transfers between devices with their start and end apart: 2 -> 0, of which waited for: 2 -> 0; matrix products, arithmetic and copies ran while one was open for 5% -> 0% of each run, Pallas kernels for 0% -> 0%
where the time goes in v1:
time: 57.9 us; the launch traced here: 57.7 us
  Pallas kernels  57 us (98%)
  between operations  0.64 us (1%)
    pallas_call x1, Pallas kernels, spectrum_call(): pl.pallas_call(functools.partial(spectrum_kernel, dims), out_shape=jax.Sh...  48.5 us
    pallas_call x1, Pallas kernels, synthesis_call(): pl.pallas_call(synthesis_kernel, grid=(NT // tile,), out_shape=(jax.Shape...  8.55 us

profile of v1, /device:TPU:1, one launch (start us, length us, event | category | flops | bytes accessed | tf_op | source)
XLA Modules:
  0.0 57.7 jit_solution(8963550131426263682)
XLA Ops:
  0.6 48.5 %spectrum.1.spec_ref = f32[2,2,32,128]{3,2,1,0:T(8,128)} custom-call(s32[16,128]{1,0:T(8,128)} %bitcast.6, s32[32]{0:T(128)} %counts_ref.1, f32[6,64]{1,0:T(8,128)} %bitcast.7, bf16[64,128,128]{2,1,0:T(8,128)(2,1)} %bitcast.5, bf16[64,2,2,6,16,128]{5,4,3,2,1,0:T(8,128)(2,1)} %sgt_hbm.1), custom_call_target="tpu_custom_call" | custom-call | tf_op jit(solution)/shard_map/spectrum/pallas_call | solution.py:330
  49.1 8.6 %synthesis.1 = (bf16[64,2048]{1,0:T(8,128)(2,1)}, f32[64,40]{1,0:T(8,128)}) custom-call(f32[2,2,32,128]{3,2,1,0:T(8,128)} %spectrum.1.spec_ref, f32[2,40,128]{2,1,0:T(8,128)} %constant.6.clone.gain_ref, bf16[256,2048]{1,0:T(8,128)(2,1)} %constant.7.clone.high_ref, bf16[256,2048]{1,0:T(8,128)(2,1)} %constant.8.clone.low_ref), custom_call_target="tpu_custom_call" | custom-call | tf_op jit(solution)/shard_map/synthesis/pallas_call | solution.py:415

commit v2 on v1

--- a/solution.py
+++ b/solution.py
@@ -11,7 +11,8 @@
 
 NT = 2048
 PERIODS = 40
-CHUNKS = 2
+HALVES = 2
+CUTS = 4
 MESH = pl.DeviceIdType.MESH
 
 damping = 0.05
@@ -47,47 +48,69 @@
 
 def spectrum_kernel(
     dims, points_ref, counts_ref, mech_ref, slip_hbm, sgt_hbm, spec_ref,
-    table, table_smem, sgt, slip, mech_out, mech_in, wide, slip_out, slip_in, flip, proj_out, proj_in,
-    pieces, piece_flip, part, part_out, part_in,
-    table_sem, sgt_sem, slip_sem, mech_ssem, mech_rsem, slip_ssem, slip_rsem, proj_ssem, proj_rsem,
+    table, table_smem, sgt, slip, mech_out, mech_in, wide, slip_out, slip_in, flip, near_out, near_in, far_out, far_in,
+    pieces, piece_flip, part, part_out, part_in, sums,
+    table_sem, sgt_sem, slip_sem, mech_ssem, mech_rsem, slip_ssem, slip_rsem, near_ssem, near_rsem, far_ssem, far_rsem,
     ring_ssem, ring_rsem, pair_ssem, pair_rsem, part_ssem, part_rsem,
 ):
     nx, nz, ny = dims
     workers = nx * nz
     slots, vq, freqs = slip.shape
-    rows_pc = 2 * 2 * sgt.shape[4]
+    sites = sgt.shape[4]
+    rows_pc = 4 * sites
     per_reader = sgt.shape[0]
     share = freqs // nx
-    group = workers // CHUNKS
+    group = workers // 2
     packs = points_ref.shape[1] // slots
     table_rows = points_ref.shape[0]
     lanes = points_ref.shape[1]
+    halves = slip_out.shape[0]
+    half = share // halves
+    cuts = far_out.shape[0]
+    cut = share // cuts
+    quads = cut // 4
 
     me = lax.axis_index("sub")
     site = lax.axis_index("site")
     my_x = me // nz
+    my_z = lax.rem(me, nz)
     my_y = site // 2
-    core = site % 2
+    core = lax.rem(site, 2)
+    other = my_y * 2 + (1 - core)
 
     get_slip = pltpu.make_async_copy(slip_hbm, slip, slip_sem)
     get_slip.start()
     get_sgt = pltpu.make_async_copy(sgt_hbm, sgt, sgt_sem)
     get_sgt.start()
 
-    def peer_of(step):
-        return lax.rem(me + step, workers)
+    def each_peer(act):
+        xs = [lax.rem(my_x + dx, nx) for dx in range(nx)]
+        order = sorted(range(nx), key=lambda dx: -min(dx, nx - dx))
+
+        @pl.loop(0, nz - 1)
+        def _(step):
+            away = (step + 1) // 2
+            dz = nz // 2 + jnp.where(lax.rem(step, 2) == 0, away, -away)
+            z = lax.rem(my_z + dz, nz)
+            place = lax.rem(nz - dz + 1, nz) * nx + my_x
+            for dx in order:
+                act(xs[dx], z, place)
+
+        for dx in order:
+            if dx:
+                act(xs[dx], my_z, nx + my_x)
+
+    my_place = nx + my_x
 
     def site_of(step):
         return lax.rem(my_y + step, ny) * 2 + core
 
-    other = my_y * 2 + (1 - core)
-
     barrier = pltpu.get_barrier_semaphore()
 
-    @pl.loop(1, workers)
-    def _(step):
-        pl.semaphore_signal(barrier, inc=1, device_id={"sub": peer_of(step)}, device_id_type=MESH)
-
+    def greet(x, z, place):
+        pl.semaphore_signal(barrier, inc=1, device_id={"sub": x * nz + z}, device_id_type=MESH)
+
+    each_peer(greet)
     for step in range(1, ny):
         pl.semaphore_signal(barrier, inc=1, device_id={"site": site_of(step)}, device_id_type=MESH)
     pl.semaphore_signal(barrier, inc=1, device_id={"site": other}, device_id_type=MESH)
@@ -138,57 +161,52 @@
     def _(zr):
         slot = table_smem[table_rows + x_of_piece * nz + zr, my_k]
         turned = slip[slot].astype(jnp.float32).T.astype(jnp.bfloat16)
-        for x in range(nx):
-            slip_out[x * nz + zr] = turned[x * share : (x + 1) * share]
-
+        for h in range(halves):
+            for x in range(nx):
+                start = x * share + h * half
+                slip_out[h, x * nz + zr] = turned[start : start + half]
+
+    get_sgt.wait()
     pl.semaphore_wait(barrier, workers - 1 + ny)
-
-    def mech_copy(peer):
-        return pltpu.make_async_remote_copy(
-            src_ref=mech_out.at[peer], dst_ref=mech_in.at[me], send_sem=mech_ssem, recv_sem=mech_rsem,
-            device_id={"sub": peer}, device_id_type=MESH,
-        )
-
-    chunk_of_me = me // group
-
-    def slip_copy(peer):
-        return pltpu.make_async_remote_copy(
-            src_ref=slip_out.at[peer], dst_ref=slip_in.at[me], send_sem=slip_ssem,
-            recv_sem=slip_rsem.at[chunk_of_me], device_id={"sub": peer}, device_id_type=MESH,
-        )
-
-    @pl.loop(1, workers)
-    def _(step):
-        mech_copy(peer_of(step)).start()
-
-    pltpu.make_async_copy(mech_out.at[me], mech_in.at[me], mech_rsem).start()
-
-    @pl.loop(1, workers)
-    def _(step):
-        slip_copy(peer_of(step)).start()
-
-    pltpu.make_async_copy(slip_out.at[me], slip_in.at[me], slip_rsem.at[chunk_of_me]).start()
 
     def wait_bytes(ref, sem):
         pltpu.make_async_copy(ref, ref, sem).wait()
 
-    get_sgt.wait()
-    wait_bytes(mech_in, mech_rsem)
-    gathered = mech_in[...].reshape(workers, 128)
-    for column in range(12):
-        wide[column] = jnp.broadcast_to(gathered[:, column : column + 1], (workers, freqs))
-
-    sites = sgt.shape[4]
-
-    def project(chunk):
-        @pl.loop(0, group)
+    def send_mech(x, z, place):
+        pltpu.make_async_remote_copy(
+            src_ref=mech_out.at[x * nz + z], dst_ref=mech_in.at[place], send_sem=mech_ssem,
+            recv_sem=mech_rsem.at[place // group], device_id={"sub": x * nz + z}, device_id_type=MESH,
+        ).start()
+
+    each_peer(send_mech)
+    pltpu.make_async_copy(mech_out.at[me], mech_in.at[my_place], mech_rsem.at[my_place // group]).start()
+
+    for h in range(halves):
+
+        def send_slip(x, z, place, h=h):
+            pltpu.make_async_remote_copy(
+                src_ref=slip_out.at[h, x * nz + z], dst_ref=slip_in.at[h, place], send_sem=slip_ssem,
+                recv_sem=slip_rsem.at[h], device_id={"sub": x * nz + z}, device_id_type=MESH,
+            ).start()
+
+        each_peer(send_slip)
+        pltpu.make_async_copy(slip_out.at[h, me], slip_in.at[h, my_place], slip_rsem.at[h]).start()
+
+    def project(turn):
+        wait_bytes(mech_in.at[pl.ds(turn * group, group)], mech_rsem.at[turn])
+        gathered = mech_in[pl.ds(turn * group, group)].reshape(group, 128)
+        for column in range(12):
+            wide[column] = jnp.broadcast_to(gathered[:, column : column + 1], (group, freqs))
+
+        @pl.loop(0, group, unroll=2)
         def _(index):
-            worker = chunk * group + index
+            place = turn * group + index
+            worker = lax.rem(place, nx) * nz + lax.rem(my_z + place // nx + nz - 1, nz)
             blocks = []
             for k in range(2):
                 point = table_smem[worker // packs, lax.rem(worker, packs) * 2 + k]
                 weights = [
-                    jnp.broadcast_to(wide[k * 6 + m, pl.ds(worker, 1), :], (sites, freqs)) for m in range(6)
+                    jnp.broadcast_to(wide[k * 6 + m, pl.ds(index, 1), :], (sites, freqs)) for m in range(6)
                 ]
                 for part_id in range(2):
                     for c in range(2):
@@ -199,117 +217,149 @@
             turned = jnp.concatenate(blocks, axis=0).T
             flip[pl.ds(index, freqs, stride=group), :] = turned
 
+    def near_copy(step):
+        x = lax.rem(my_x + step, nx)
+        return pltpu.make_async_remote_copy(
+            src_ref=near_out.at[x], dst_ref=near_in.at[my_x], send_sem=near_ssem, recv_sem=near_rsem,
+            device_id={"sub": x * nz + my_z}, device_id_type=MESH,
+        )
+
+    def far_copy(i, step):
+        x = lax.rem(my_x + step, nx)
+        return pltpu.make_async_remote_copy(
+            src_ref=far_out.at[i, x], dst_ref=far_in.at[i, my_x], send_sem=far_ssem.at[i],
+            recv_sem=far_rsem.at[i], device_id={"sub": x * nz + my_z}, device_id_type=MESH,
+        )
+
+    def ring_copy(h, step):
+        piece = pieces.at[h, site]
+        return pltpu.make_async_remote_copy(
+            src_ref=piece, dst_ref=piece, send_sem=ring_ssem.at[h, step - 1],
+            recv_sem=ring_rsem.at[h, step - 1], device_id={"site": site_of(step)}, device_id_type=MESH,
+        )
+
+    def pair_copy(h, y):
+        piece = pieces.at[h, y * 2 + core]
+        return pltpu.make_async_remote_copy(
+            src_ref=piece, dst_ref=piece, send_sem=pair_ssem.at[h], recv_sem=pair_rsem.at[h],
+            device_id={"site": other}, device_id_type=MESH,
+        )
+
+    hops = sorted(range(1, nx), key=lambda dx: -min(dx, nx - dx))
+
+    def send_near():
         for x in range(nx):
             rows = share * group
-            block = flip[pl.ds(x * rows, rows), :].astype(jnp.bfloat16)
-            proj_out[chunk, x] = block.reshape(share, group, 2 * rows_pc)
-        for step in range(1, nx):
-            proj_copy(chunk, step).start()
-        pltpu.make_async_copy(proj_out.at[chunk, my_x], proj_in.at[chunk, my_x], proj_rsem.at[chunk]).start()
-
-    my_z = lax.rem(me, nz)
-
-    def proj_copy(chunk, step):
-        x = lax.rem(my_x + step, nx)
-        return pltpu.make_async_remote_copy(
-            src_ref=proj_out.at[chunk, x], dst_ref=proj_in.at[chunk, my_x], send_sem=proj_ssem.at[chunk],
-            recv_sem=proj_rsem.at[chunk], device_id={"sub": x * nz + my_z}, device_id_type=MESH,
-        )
-
-    def ring_copy(chunk, step):
-        piece = pieces.at[chunk, site]
-        return pltpu.make_async_remote_copy(
-            src_ref=piece, dst_ref=piece, send_sem=ring_ssem.at[chunk, step - 1],
-            recv_sem=ring_rsem.at[chunk, step - 1], device_id={"site": site_of(step)}, device_id_type=MESH,
-        )
-
-    def pair_copy(chunk, y):
-        piece = pieces.at[chunk, y * 2 + core]
-        return pltpu.make_async_remote_copy(
-            src_ref=piece, dst_ref=piece, send_sem=pair_ssem.at[chunk], recv_sem=pair_rsem.at[chunk],
-            device_id={"site": other}, device_id_type=MESH,
-        )
-
-    def share_slip(chunk):
-        wait_bytes(slip_in.at[pl.ds(chunk * group, group)], slip_rsem.at[chunk])
-        for index in range(group):
-            piece_flip[pl.ds(index, share, stride=group), :] = slip_in[chunk * group + index].astype(jnp.float32)
-        pieces[chunk, site] = piece_flip[...].astype(jnp.bfloat16).reshape(share, group, vq)
+            near_out[x] = flip[pl.ds(x * rows, rows), :].astype(jnp.bfloat16).reshape(share, group, 2 * rows_pc)
+        for step in hops:
+            near_copy(step).start()
+        pltpu.make_async_copy(near_out.at[my_x], near_in.at[my_x], near_rsem).start()
+
+    def send_far():
+        for i in range(cuts):
+            for x in range(nx):
+                rows = cut * group
+                block = flip[pl.ds((x * cuts + i) * rows, rows), :].astype(jnp.bfloat16)
+                far_out[i, x] = block.reshape(cut, group, 2 * rows_pc)
+            for step in hops:
+                far_copy(i, step).start()
+            pltpu.make_async_copy(far_out.at[i, my_x], far_in.at[i, my_x], far_rsem.at[i]).start()
+
+    def share_slip(h):
+        wait_bytes(slip_in.at[h], slip_rsem.at[h])
+        for place in range(workers):
+            piece_flip[pl.ds(place, half, stride=workers), :] = slip_in[h, place].astype(jnp.float32)
+        pieces[h, site] = piece_flip[...].astype(jnp.bfloat16).reshape(half, workers, vq)
         for step in range(1, ny):
-            ring_copy(chunk, step).start()
-        pair_copy(chunk, my_y).start()
-
-    for chunk in range(CHUNKS):
-        project(chunk)
-        share_slip(chunk)
-    for chunk in range(CHUNKS):
+            ring_copy(h, step).start()
+        pair_copy(h, my_y).start()
+
+    def pass_on(h):
         for step in range(1, ny):
             y = lax.rem(my_y + ny - step, ny)
-            wait_bytes(pieces.at[chunk, y * 2 + core], ring_rsem.at[chunk, step - 1])
-            pair_copy(chunk, y).start()
-    for chunk in range(CHUNKS):
-        wait_bytes(proj_in.at[chunk], proj_rsem.at[chunk])
-        wait_bytes(pieces.at[chunk, pl.ds(0, ny)], pair_rsem.at[chunk])
-
-    quads = share // 4
+            wait_bytes(pieces.at[h, y * 2 + core], ring_rsem.at[h, step - 1])
+            pair_copy(h, y).start()
+
     lane = lax.broadcasted_iota(jnp.int32, (rows_pc // 2, vq), 1)
     even = lane % 2 == 0
 
-    @pl.loop(0, quads)
-    def _(quad):
-        blocks = []
-        for inner in range(4):
-            f = quad * 4 + inner
-            projected = jnp.concatenate(
-                [proj_in[chunk, x, f] for chunk in range(CHUNKS) for x in range(nx)], axis=0
-            ).T
-            left = jnp.concatenate([projected[:rows_pc], projected[rows_pc:]], axis=1)
-            right = jnp.concatenate(
-                [pieces[chunk, k * nx + x, f] for k in range(2) for chunk in range(CHUNKS) for x in range(nx)], axis=0
-            )
-            both = jnp.dot(left, right, preferred_element_type=jnp.float32)
-            straight, crossed = both[: rows_pc // 2], both[rows_pc // 2 :]
-            swapped = jnp.where(even, -pltpu.roll(crossed, vq - 1, 1), pltpu.roll(crossed, 1, 1))
-            blocks.append(straight + swapped)
-        part[pl.ds(quad, vq, stride=quads), :] = jnp.concatenate(blocks, axis=0).T
-
-    width = 4 * quads
-    part_out[...] = part[...].astype(jnp.bfloat16).reshape(workers, width, 128)
-
-    def part_copy(peer):
-        return pltpu.make_async_remote_copy(
-            src_ref=part_out.at[peer], dst_ref=part_in.at[me], send_sem=part_ssem, recv_sem=part_rsem,
-            device_id={"sub": peer}, device_id_type=MESH,
-        )
-
-    @pl.loop(1, workers)
-    def _(step):
-        part_copy(peer_of(step)).start()
-
-    pltpu.make_async_copy(part_out.at[me], part_in.at[me], part_rsem).start()
+    def contract(i):
+        wait_bytes(far_in.at[i], far_rsem.at[i])
+        for quad in range(quads):
+            blocks = []
+            for inner in range(4):
+                f = quad * 4 + inner
+                whole = i * cut + f
+                projected = jnp.concatenate(
+                    [near_in[x, whole] for x in range(nx)] + [far_in[i, x, f] for x in range(nx)], axis=0
+                ).T
+                left = jnp.concatenate([projected[:rows_pc], projected[rows_pc:]], axis=1)
+                right = jnp.concatenate(
+                    [
+                        pieces[whole // half, k * nx + x, whole % half, pl.ds(turn * group, group), :]
+                        for k in range(2)
+                        for turn in range(2)
+                        for x in range(nx)
+                    ],
+                    axis=0,
+                )
+                both = jnp.dot(left, right, preferred_element_type=jnp.float32)
+                straight, crossed = both[: rows_pc // 2], both[rows_pc // 2 :]
+                swapped = jnp.where(even, -pltpu.roll(crossed, vq - 1, 1), pltpu.roll(crossed, 1, 1))
+                blocks.append(straight + swapped)
+            part[i, pl.ds(quad, vq, stride=quads), :] = jnp.concatenate(blocks, axis=0).T
+        part_out[i] = part[i].astype(jnp.bfloat16).reshape(workers, 4 * quads, 128)
+
+        def send_part(x, z, place):
+            pltpu.make_async_remote_copy(
+                src_ref=part_out.at[i, x * nz + z], dst_ref=part_in.at[i, me], send_sem=part_ssem,
+                recv_sem=part_rsem.at[i], device_id={"sub": x * nz + z}, device_id_type=MESH,
+            ).start()
+
+        each_peer(send_part)
+        pltpu.make_async_copy(part_out.at[i, me], part_in.at[i, me], part_rsem.at[i]).start()
+
+    project(0)
+    send_near()
+    share_slip(0)
+    project(1)
+    send_far()
+    for h in range(1, halves):
+        share_slip(h)
+    pass_on(0)
+    wait_bytes(near_in, near_rsem)
+    for i in range(cuts):
+        if i % (cuts // halves) == 0:
+            h = i // (cuts // halves)
+            if h:
+                pass_on(h)
+            wait_bytes(pieces.at[h, pl.ds(0, ny)], pair_rsem.at[h])
+        contract(i)
 
     wait_bytes(mech_out.at[pl.ds(0, workers - 1)], mech_ssem)
-    wait_bytes(slip_out.at[pl.ds(0, workers - 1)], slip_ssem)
-    for chunk in range(CHUNKS):
-        wait_bytes(proj_out.at[chunk, pl.ds(0, nx - 1)], proj_ssem.at[chunk])
+    wait_bytes(slip_out.at[:, pl.ds(0, workers - 1)], slip_ssem)
+    wait_bytes(near_out.at[pl.ds(0, nx - 1)], near_ssem)
+    for i in range(cuts):
+        wait_bytes(far_out.at[i, pl.ds(0, nx - 1)], far_ssem.at[i])
+    for h in range(halves):
         for step in range(1, ny):
-            wait_bytes(pieces.at[chunk, site], ring_ssem.at[chunk, step - 1])
-        wait_bytes(pieces.at[chunk, pl.ds(0, ny)], pair_ssem.at[chunk])
-    wait_bytes(part_in, part_rsem)
-    wait_bytes(part_out.at[pl.ds(0, workers - 1)], part_ssem)
-
-    totals = []
-    for x in range(nx):
-        total = part_in[x * nz].astype(jnp.float32)
-        for z in range(1, nz):
-            total = total + part_in[x * nz + z].astype(jnp.float32)
-        totals.append(total)
+            wait_bytes(pieces.at[h, site], ring_ssem.at[h, step - 1])
+        wait_bytes(pieces.at[h, pl.ds(0, ny)], pair_ssem.at[h])
+
+    for i in range(cuts):
+        wait_bytes(part_in.at[i], part_rsem.at[i])
+        for x in range(nx):
+            total = part_in[i, x * nz].astype(jnp.float32)
+            for z in range(1, nz):
+                total = total + part_in[i, x * nz + z].astype(jnp.float32)
+            for row in range(4):
+                sums[row, pl.ds((x * cuts + i) * quads, quads), :] = total[row * quads : (row + 1) * quads]
+    rows = rows_pc // 2
     for e in range(2):
         for q in range(2):
-            start = (e * 2 + q) * quads
-            turned = jnp.concatenate([total[start : start + quads] for total in totals], axis=0).T
-            rows = rows_pc // 2
+            turned = sums[e * 2 + q].T
             spec_ref[e, q] = jnp.concatenate([turned[i * rows : (i + 1) * rows] for i in range(4)], axis=1)
+    wait_bytes(part_out.at[:, pl.ds(0, workers - 1)], part_ssem)
 
 
 def spectrum_call(dims, sgt, mechanism, slip, point_list, subfault_counts):
@@ -319,11 +369,12 @@
     vq = variations * 2
     rows_pc = 4 * sgt.shape[4]
     share = freqs // nx
-    group = workers // CHUNKS
+    group = workers // 2
+    half, cut = share // HALVES, share // CUTS
+    quads = cut // 4
     packs = max(1, min(128 // slots, 2))
     table_rows = workers // packs
     points = point_list.reshape(table_rows, packs * slots)
-    width = share
     bf16, f32 = jnp.bfloat16, jnp.float32
     dma = pltpu.SemaphoreType.DMA
     vmem, smem, anywhere = (pl.BlockSpec(memory_space=s) for s in (pltpu.VMEM, pltpu.SMEM, pl.ANY))
@@ -339,19 +390,22 @@
             pltpu.VMEM((slots, vq, freqs), bf16),
             pltpu.VMEM((workers, 1, 128), f32),
             pltpu.VMEM((workers, 1, 128), f32),
-            pltpu.VMEM((12, workers, freqs), f32),
-            pltpu.VMEM((workers, share, vq), bf16),
-            pltpu.VMEM((workers, share, vq), bf16),
+            pltpu.VMEM((12, group, freqs), f32),
+            pltpu.VMEM((HALVES, workers, half, vq), bf16),
+            pltpu.VMEM((HALVES, workers, half, vq), bf16),
             pltpu.VMEM((freqs * group, 2 * rows_pc), f32),
-            pltpu.VMEM((CHUNKS, nx, share, group, 2 * rows_pc), bf16),
-            pltpu.VMEM((CHUNKS, nx, share, group, 2 * rows_pc), bf16),
-            pltpu.VMEM((CHUNKS, ny * 2, share, group, vq), bf16),
-            pltpu.VMEM((share * group, vq), f32),
-            pltpu.VMEM((workers * width, 128), f32),
-            pltpu.VMEM((workers, width, 128), bf16),
-            pltpu.VMEM((workers, width, 128), bf16),
-            dma, dma, dma, dma, dma, dma, dma((CHUNKS,)), dma((CHUNKS,)), dma((CHUNKS,)),
-            dma((CHUNKS, ny - 1)), dma((CHUNKS, ny - 1)), dma((CHUNKS,)), dma((CHUNKS,)), dma, dma,
+            pltpu.VMEM((nx, share, group, 2 * rows_pc), bf16),
+            pltpu.VMEM((nx, share, group, 2 * rows_pc), bf16),
+            pltpu.VMEM((CUTS, nx, cut, group, 2 * rows_pc), bf16),
+            pltpu.VMEM((CUTS, nx, cut, group, 2 * rows_pc), bf16),
+            pltpu.VMEM((HALVES, ny * 2, half, workers, vq), bf16),
+            pltpu.VMEM((half * workers, vq), f32),
+            pltpu.VMEM((CUTS, vq * quads, 128), f32),
+            pltpu.VMEM((CUTS, workers, 4 * quads, 128), bf16),
+            pltpu.VMEM((CUTS, workers, 4 * quads, 128), bf16),
+            pltpu.VMEM((4, share // 4 * nx, 128), f32),
+            dma, dma, dma, dma, dma((2,)), dma, dma((HALVES,)), dma, dma, dma((CUTS,)), dma((CUTS,)),
+            dma((HALVES, ny - 1)), dma((HALVES, ny - 1)), dma((HALVES,)), dma((HALVES,)), dma, dma((CUTS,)),
         ],
         compiler_params=pltpu.CompilerParams(
             collective_id=0, has_side_effects=True, vmem_limit_bytes=63 * 1024 * 1024

time: 57.9 us -> 51.2 us (0.88)
  Pallas kernels: 57 us -> 50.2 us
    pallas_call x1, Pallas kernels: 48.5 us -> 41.8 us  [spectrum_call(): pl.pallas_call(functools.partial(spectrum_kernel, dims), out_shape=jax.Sh...]
where the time goes in v2:
time: 51.2 us; the launch traced here: 50.9 us
  Pallas kernels  50.2 us (98%)
  between operations  0.64 us (1%)
    pallas_call x1, Pallas kernels, spectrum_call(): pl.pallas_call(functools.partial(spectrum_kernel, dims), out_shape=jax.Sh...  41.8 us
    pallas_call x1, Pallas kernels, synthesis_call(): pl.pallas_call(synthesis_kernel, grid=(NT // tile,), out_shape=(jax.Shape...  8.49 us

profile of v2, /device:TPU:1, one launch (start us, length us, event | category | flops | bytes accessed | tf_op | source)
XLA Modules:
  0.0 50.9 jit_solution(16583621448853541980)
XLA Ops:
  0.6 41.8 %spectrum.1.spec_ref = f32[2,2,32,128]{3,2,1,0:T(8,128)} custom-call(s32[16,128]{1,0:T(8,128)} %bitcast.6, s32[32]{0:T(128)} %counts_ref.1, f32[6,64]{1,0:T(8,128)} %bitcast.7, bf16[64,128,128]{2,1,0:T(8,128)(2,1)} %bitcast.5, bf16[64,2,2,6,16,128]{5,4,3,2,1,0:T(8,128)(2,1)} %sgt_hbm.1), custom_call_target="tpu_custom_call" | custom-call | tf_op jit(solution)/shard_map/spectrum/pallas_call | solution.py:381
  42.4 8.5 %synthesis.1 = (bf16[64,2048]{1,0:T(8,128)(2,1)}, f32[64,40]{1,0:T(8,128)}) custom-call(f32[2,2,32,128]{3,2,1,0:T(8,128)} %spectrum.1.spec_ref, f32[2,40,128]{2,1,0:T(8,128)} %constant.6.clone.gain_ref, bf16[256,2048]{1,0:T(8,128)(2,1)} %constant.7.clone.high_ref, bf16[256,2048]{1,0:T(8,128)(2,1)} %constant.8.clone.low_ref), custom_call_target="tpu_custom_call" | custom-call | tf_op jit(solution)/shard_map/synthesis/pallas_call | solution.py:469

commit v3 on v2

--- a/solution.py
+++ b/solution.py
@@ -13,6 +13,8 @@
 PERIODS = 40
 HALVES = 2
 CUTS = 4
+PARTS = 5
+TILE = 512
 MESH = pl.DeviceIdType.MESH
 
 damping = 0.05
@@ -47,10 +49,10 @@
 
 
 def spectrum_kernel(
-    dims, points_ref, counts_ref, mech_ref, slip_hbm, sgt_hbm, spec_ref,
-    table, table_smem, sgt, slip, mech_out, mech_in, wide, slip_out, slip_in, flip, near_out, near_in, far_out, far_in,
+    dims, points_hbm, counts_hbm, mech_hbm, slip_hbm, sgt_hbm, spec_ref,
+    points_ref, counts_ref, mech_ref, table, table_smem, sgt, slip, mech_out, mech_in, wide, slip_out, slip_in, flip, near_out, near_in, far_out, far_in,
     pieces, piece_flip, part, part_out, part_in, sums,
-    table_sem, sgt_sem, slip_sem, mech_ssem, mech_rsem, slip_ssem, slip_rsem, near_ssem, near_rsem, far_ssem, far_rsem,
+    small_sem, table_sem, sgt_sem, slip_sem, mech_ssem, mech_rsem, slip_ssem, slip_rsem, near_ssem, near_rsem, far_ssem, far_rsem,
     ring_ssem, ring_rsem, pair_ssem, pair_rsem, part_ssem, part_rsem,
 ):
     nx, nz, ny = dims
@@ -78,6 +80,14 @@
     core = lax.rem(site, 2)
     other = my_y * 2 + (1 - core)
 
+    small = [
+        pltpu.make_async_copy(source, target, small_sem.at[i])
+        for i, (source, target) in enumerate(
+            ((points_hbm, points_ref), (counts_hbm, counts_ref), (mech_hbm, mech_ref))
+        )
+    ]
+    for copy in small:
+        copy.start()
     get_slip = pltpu.make_async_copy(slip_hbm, slip, slip_sem)
     get_slip.start()
     get_sgt = pltpu.make_async_copy(sgt_hbm, sgt, sgt_sem)
@@ -115,6 +125,8 @@
         pl.semaphore_signal(barrier, inc=1, device_id={"site": site_of(step)}, device_id_type=MESH)
     pl.semaphore_signal(barrier, inc=1, device_id={"site": other}, device_id_type=MESH)
 
+    for copy in small:
+        copy.wait()
     points = points_ref[...]
     lane = lax.broadcasted_iota(jnp.int32, (table_rows, lanes), 1)
     out_lane = lax.broadcasted_iota(jnp.int32, (table_rows, 128), 1)
@@ -377,13 +389,17 @@
     points = point_list.reshape(table_rows, packs * slots)
     bf16, f32 = jnp.bfloat16, jnp.float32
     dma = pltpu.SemaphoreType.DMA
-    vmem, smem, anywhere = (pl.BlockSpec(memory_space=s) for s in (pltpu.VMEM, pltpu.SMEM, pl.ANY))
+    hbm = pl.BlockSpec(memory_space=pltpu.HBM)
+    operands = (points, subfault_counts, mechanism.T, slip.reshape(slots, vq, freqs), sgt)
     return pl.pallas_call(
         functools.partial(spectrum_kernel, dims),
         out_shape=jax.ShapeDtypeStruct((2, 2, rows_pc // 2, freqs), f32),
-        in_specs=[vmem, smem, vmem, anywhere, anywhere],
-        out_specs=vmem,
+        in_specs=[hbm] * 5,
+        out_specs=pl.BlockSpec(memory_space=pltpu.VMEM),
         scratch_shapes=[
+            pltpu.VMEM(points.shape, jnp.int32),
+            pltpu.SMEM(subfault_counts.shape, jnp.int32),
+            pltpu.VMEM((6, slots), f32),
             pltpu.VMEM((table_rows + workers, 128), jnp.int32),
             pltpu.SMEM((table_rows + workers, 128), jnp.int32),
             pltpu.VMEM(sgt.shape, bf16),
@@ -404,91 +420,109 @@
             pltpu.VMEM((CUTS, workers, 4 * quads, 128), bf16),
             pltpu.VMEM((CUTS, workers, 4 * quads, 128), bf16),
             pltpu.VMEM((4, share // 4 * nx, 128), f32),
-            dma, dma, dma, dma, dma((2,)), dma, dma((HALVES,)), dma, dma, dma((CUTS,)), dma((CUTS,)),
+            dma((3,)), dma, dma, dma, dma, dma((2,)), dma, dma((HALVES,)), dma, dma, dma((CUTS,)), dma((CUTS,)),
             dma((HALVES, ny - 1)), dma((HALVES, ny - 1)), dma((HALVES,)), dma((HALVES,)), dma, dma((CUTS,)),
         ],
         compiler_params=pltpu.CompilerParams(
-            collective_id=0, has_side_effects=True, vmem_limit_bytes=63 * 1024 * 1024
+            collective_id=0, has_side_effects=True, vmem_limit_bytes=36 * 1024 * 1024
         ),
         name="spectrum",
-    )(points, subfault_counts, mechanism.T, slip.reshape(slots, vq, freqs), sgt)
-
-
-def synthesis_kernel(spec_ref, gain_ref, high_ref, low_ref, seis_ref, psa_ref, response, source, peak):
-    step = pl.program_id(0)
-    periods = gain_ref.shape[1]
-    freqs = gain_ref.shape[2]
-    rows = source.shape[1]
-
-    @pl.when(step == 0)
-    def _():
-        real = jnp.concatenate([spec_ref[0, 0], spec_ref[1, 0]], axis=0)
-        imag = jnp.concatenate([spec_ref[0, 1], spec_ref[1, 1]], axis=0)
-        spectrum = jnp.concatenate([real, imag], axis=1)
-        top = spectrum.astype(jnp.bfloat16)
-        source[0] = top
-        source[1] = (spectrum - top.astype(jnp.float32)).astype(jnp.bfloat16)
-        for q in range(periods):
+    )(*(pltpu.with_memory_space_constraint(x, pltpu.HBM) for x in operands))
+
+
+def synthesis_kernel(
+    spec_ref, gain_ref, high, low, seis_hbm, psa_ref, rows_in, peak, seis, put_sem
+):
+    tiles, _, tile = high.shape
+    periods, freqs = gain_ref.shape[1:]
+    rows = spec_ref.shape[2] * 2
+    pair = 2 * rows
+    per = periods // PARTS
+
+    def put(t):
+        return pltpu.make_async_copy(seis.at[t], seis_hbm.at[:, pl.ds(t * tile, tile)], put_sem.at[t])
+
+
+    real = jnp.concatenate([spec_ref[0, 0], spec_ref[1, 0]], axis=0)
+    imag = jnp.concatenate([spec_ref[0, 1], spec_ref[1, 1]], axis=0)
+    spectrum = jnp.concatenate([real, imag], axis=1)
+    top = spectrum.astype(jnp.bfloat16)
+    rows_in[pl.ds(0, rows), :] = top
+    rows_in[pl.ds(rows, rows), :] = (spectrum - top.astype(jnp.float32)).astype(jnp.bfloat16)
+
+    def respond(start):
+        for place in range(start, start + per):
+            q = place // 2 + (place % 2) * (periods // 2)
             g0 = gain_ref[0, q : q + 1, :]
             g1 = gain_ref[1, q : q + 1, :]
-            response[pl.ds(q * rows, rows), pl.ds(0, freqs)] = (g0 * real - g1 * imag).astype(jnp.bfloat16)
-            response[pl.ds(q * rows, rows), pl.ds(freqs, freqs)] = (g0 * imag + g1 * real).astype(jnp.bfloat16)
-        peak[...] = jnp.zeros_like(peak)
-
-    high = high_ref[...]
-    motion = (
-        jnp.dot(source[0], high, preferred_element_type=jnp.float32)
-        + jnp.dot(source[1], high, preferred_element_type=jnp.float32)
-        + jnp.dot(source[0], low_ref[...], preferred_element_type=jnp.float32)
-    )
-    seis_ref[...] = motion.astype(jnp.bfloat16)
-    per = 8
-    for start in range(0, periods, per):
-        part = pl.ds(start * rows, per * rows)
-        wave = jnp.abs(jnp.dot(response[part, :], high, preferred_element_type=jnp.float32))
-        most = peak[part, :]
-        for t in range(0, wave.shape[1], 128):
-            most = jnp.maximum(most, wave[:, t : t + 128])
-        peak[part, :] = most
-
-    @pl.when(step == pl.num_programs(0) - 1)
-    def _():
-        lane = lax.broadcasted_iota(jnp.int32, (rows, periods), 1)
-        total = jnp.zeros((rows, periods), jnp.float32)
-        for q in range(periods):
-            most = jnp.max(peak[pl.ds(q * rows, rows), :], axis=1, keepdims=True)
-            total = jnp.where(lane == q, most, total)
-        psa_ref[...] = total
+            at = pl.ds(pair + place * rows, rows)
+            rows_in[at, pl.ds(0, freqs)] = (g0 * real - g1 * imag).astype(jnp.bfloat16)
+            rows_in[at, pl.ds(freqs, freqs)] = (g0 * imag + g1 * real).astype(jnp.bfloat16)
+
+    def tile_step(t, opening=False, closing=False):
+        found = []
+        for start in range(0, periods, per):
+            if opening:
+                respond(start)
+            first = 0 if start == 0 else pair + start * rows
+            last = pair + (start + per) * rows
+            wave = jnp.dot(rows_in[first:last, :], high[t], preferred_element_type=jnp.float32)
+            if start == 0:
+                motion = wave[:rows] + wave[rows:pair]
+                motion = motion + jnp.dot(rows_in[:rows, :], low[t], preferred_element_type=jnp.float32)
+                seis[t] = motion.astype(jnp.bfloat16)
+                wave = wave[pair:]
+            wave = jnp.abs(wave)
+            most = wave[:, :128]
+            for column in range(128, tile, 128):
+                most = jnp.maximum(most, wave[:, column : column + 128])
+            part = pl.ds(start * rows, per * rows)
+            if not opening:
+                most = jnp.maximum(peak[part, :], most)
+            if not closing:
+                peak[part, :] = most
+            else:
+                for block in range(0, per * rows, pair):
+                    found.append(jnp.max(most[block : block + pair].T, axis=0, keepdims=True))
+        put(t).start()
+        return found
+
+    tile_step(0, opening=True)
+
+    @pl.loop(1, tiles - 1)
+    def _(t):
+        tile_step(t)
+
+    found = tile_step(tiles - 1, closing=True)
+    both = jnp.concatenate(found, axis=0)
+    psa_ref[...] = jnp.concatenate([both[:, :rows].T, both[:, rows:].T], axis=1)
+    for t in range(tiles):
+        put(t).wait()
 
 
 def synthesis_call(spec):
     rows, freqs = 2 * spec.shape[2], spec.shape[3]
-    high, low = synthesis_basis(freqs, NT)
+    high, low = (
+        np.ascontiguousarray(a.reshape(2 * freqs, NT // TILE, TILE).swapaxes(0, 1)) for a in synthesis_basis(freqs, NT)
+    )
     gains = oscillator_gains(PERIODS, freqs, NT)
-    tile = 256
+    tiles = NT // TILE
+    vmem, anywhere = pl.BlockSpec(memory_space=pltpu.VMEM), pl.BlockSpec(memory_space=pl.ANY)
     return pl.pallas_call(
         synthesis_kernel,
-        grid=(NT // tile,),
         out_shape=(
             jax.ShapeDtypeStruct((rows, NT), jnp.bfloat16),
             jax.ShapeDtypeStruct((rows, PERIODS), jnp.float32),
         ),
-        in_specs=[
-            pl.BlockSpec(spec.shape, lambda t: (0, 0, 0, 0)),
-            pl.BlockSpec(gains.shape, lambda t: (0, 0, 0)),
-            pl.BlockSpec((2 * freqs, tile), lambda t: (0, t)),
-            pl.BlockSpec((2 * freqs, tile), lambda t: (0, t)),
+        in_specs=[vmem, vmem, vmem, vmem],
+        out_specs=(anywhere, vmem),
+        scratch_shapes=[
+            pltpu.VMEM(((PERIODS + 2) * rows, 2 * freqs), jnp.bfloat16),
+            pltpu.VMEM((PERIODS * rows, 128), jnp.float32),
+            pltpu.VMEM((tiles, rows, TILE), jnp.bfloat16),
+            pltpu.SemaphoreType.DMA((tiles,)),
         ],
-        out_specs=(
-            pl.BlockSpec((rows, tile), lambda t: (0, t)),
-            pl.BlockSpec((rows, PERIODS), lambda t: (0, 0)),
-        ),
-        scratch_shapes=[
-            pltpu.VMEM((PERIODS * rows, 2 * freqs), jnp.bfloat16),
-            pltpu.VMEM((2, rows, 2 * freqs), jnp.bfloat16),
-            pltpu.VMEM((PERIODS * rows, 128), jnp.float32),
-        ],
-        compiler_params=pltpu.CompilerParams(dimension_semantics=("arbitrary",)),
+        compiler_params=pltpu.CompilerParams(vmem_limit_bytes=36 * 1024 * 1024),
         name="synthesis",
     )(spec, jnp.asarray(gains), jnp.asarray(high), jnp.asarray(low))
 

time: 51.2 us -> 46.4 us (0.906)
  Pallas kernels: 50.2 us -> 45.6 us
    pallas_call x1, Pallas kernels: 8.49 us -> 4.77 us  [synthesis_call(): pl.pallas_call(synthesis_kernel, out_shape=(jax.ShapeDtypeStruct((rows, N...]
    pallas_call x1, Pallas kernels: 41.8 us -> 40.8 us  [spectrum_call(): pl.pallas_call(functools.partial(spectrum_kernel, dims), out_shape=jax.Sh...]
where the time goes in v3:
time: 46.4 us; the launch traced here: 46.3 us
  Pallas kernels  45.6 us (98%)
  between operations  0.69 us (1%)
    pallas_call x1, Pallas kernels, spectrum_call(): pl.pallas_call(functools.partial(spectrum_kernel, dims), out_shape=jax.Sh...  40.8 us
    pallas_call x1, Pallas kernels, synthesis_call(): pl.pallas_call(synthesis_kernel, out_shape=(jax.ShapeDtypeStruct((rows, N...  4.77 us

profile of v3, /device:TPU:1, one launch (start us, length us, event | category | flops | bytes accessed | tf_op | source)
XLA Modules:
  0.0 46.3 jit_solution(10050536756065573195)
XLA Ops:
  0.6 0.0 copy-start
  0.6 0.0 copy-start.1
  0.7 0.0 copy-start.2
  0.7 40.8 %spectrum.1.spec_ref = f32[2,2,32,128]{3,2,1,0:T(8,128)S(1)} custom-call(s32[16,128]{1,0:T(8,128)} %bitcast.6, s32[32]{0:T(128)} %counts_hbm.1, f32[6,64]{1,0:T(8,128)} %bitcast.7, bf16[64,128,128]{2,1,0:T(8,128)(2,1)} %bitcast.5, bf16[64,2,2,6,16,128]{5,4,3,2,1,0:T(8,128)(2,1)} %sgt_hbm.1), custom_call_target="tpu_custom_call" | custom-call | tf_op jit(solution)/shard_map/spectrum/pallas_call | solution.py:394
  41.5 0.0 copy-done
  41.5 0.0 copy-done.1
  41.5 0.0 copy-done.2
  41.5 4.8 %synthesis.1 = (bf16[64,2048]{1,0:T(8,128)(2,1)}, f32[64,40]{1,0:T(8,128)}) custom-call(f32[2,2,32,128]{3,2,1,0:T(8,128)S(1)} %spectrum.1.spec_ref, f32[2,40,128]{2,1,0:T(8,128)S(1)} %copy-done.2, bf16[4,256,512]{2,1,0:T(8,128)(2,1)S(1)} %copy-done.1, bf16[4,256,512]{2,1,0:T(8,128)(2,1)S(1)} %copy-done), custom_call_target="tpu_custom_call" | custom-call | tf_op jit(solution)/shard_map/synthesis/pallas_call | solution.py:511
Async XLA Ops:
  0.6 40.9 %copy-start = (bf16[4,256,512]{2,1,0:T(8,128)(2,1)S(1)}, bf16[4,256,512]{2,1,0:T(8,128)(2,1)}, u32[]{:S(2)}) copy-start(bf16[4,256,512]{2,1,0:T(8,128)(2,1)} %constant.8.clone.low) | copy-start | bytes 3145732
  0.6 40.9 %copy-start.1 = (bf16[4,256,512]{2,1,0:T(8,128)(2,1)S(1)}, bf16[4,256,512]{2,1,0:T(8,128)(2,1)}, u32[]{:S(2)}) copy-start(bf16[4,256,512]{2,1,0:T(8,128)(2,1)} %constant.7.clone.high) | copy-start | bytes 3145732
  0.7 40.9 %copy-start.2 = (f32[2,40,128]{2,1,0:T(8,128)S(1)}, f32[2,40,128]{2,1,0:T(8,128)}, u32[]{:S(2)}) copy-start(f32[2,40,128]{2,1,0:T(8,128)} %constant.6.clone.gain_ref) | copy-start | bytes 122884

commit v4 on v3

--- a/solution.py
+++ b/solution.py
@@ -11,7 +11,8 @@
 
 NT = 2048
 PERIODS = 40
-HALVES = 2
+HALVES = 4
+DEPTH = 2
 CUTS = 4
 PARTS = 5
 TILE = 512
@@ -210,7 +211,7 @@
         for column in range(12):
             wide[column] = jnp.broadcast_to(gathered[:, column : column + 1], (group, freqs))
 
-        @pl.loop(0, group, unroll=2)
+        @pl.loop(0, group, unroll=4)
         def _(index):
             place = turn * group + index
             worker = lax.rem(place, nx) * nz + lax.rem(my_z + place // nx + nz - 1, nz)
@@ -282,12 +283,22 @@
         for place in range(workers):
             piece_flip[pl.ds(place, half, stride=workers), :] = slip_in[h, place].astype(jnp.float32)
         pieces[h, site] = piece_flip[...].astype(jnp.bfloat16).reshape(half, workers, vq)
-        for step in range(1, ny):
+        pair_copy(h, my_y).start()
+
+    ring_steps = sorted(range(1, ny), key=lambda dy: -min(dy, ny - dy))
+
+    def sent_ring(h):
+        for step in ring_steps:
+            wait_bytes(pieces.at[h, site], ring_ssem.at[h, step - 1])
+
+    def launch(h):
+        if h >= DEPTH:
+            sent_ring(h - DEPTH)
+        for step in ring_steps:
             ring_copy(h, step).start()
-        pair_copy(h, my_y).start()
 
     def pass_on(h):
-        for step in range(1, ny):
+        for step in reversed(ring_steps):
             y = lax.rem(my_y + ny - step, ny)
             wait_bytes(pieces.at[h, y * 2 + core], ring_rsem.at[h, step - 1])
             pair_copy(h, y).start()
@@ -334,16 +345,21 @@
     project(0)
     send_near()
     share_slip(0)
+    launch(0)
     project(1)
     send_far()
     for h in range(1, halves):
         share_slip(h)
-    pass_on(0)
+        if h < DEPTH:
+            launch(h)
+    for h in range(DEPTH, halves):
+        launch(h)
+        pass_on(h - DEPTH)
     wait_bytes(near_in, near_rsem)
     for i in range(cuts):
         if i % (cuts // halves) == 0:
             h = i // (cuts // halves)
-            if h:
+            if h >= halves - DEPTH:
                 pass_on(h)
             wait_bytes(pieces.at[h, pl.ds(0, ny)], pair_rsem.at[h])
         contract(i)
@@ -354,8 +370,8 @@
     for i in range(cuts):
         wait_bytes(far_out.at[i, pl.ds(0, nx - 1)], far_ssem.at[i])
     for h in range(halves):
-        for step in range(1, ny):
-            wait_bytes(pieces.at[h, site], ring_ssem.at[h, step - 1])
+        if h >= halves - DEPTH:
+            sent_ring(h)
         wait_bytes(pieces.at[h, pl.ds(0, ny)], pair_ssem.at[h])
 
     for i in range(cuts):

time: 46.4 us -> 44.6 us (0.961)
  Pallas kernels: 45.6 us -> 43.8 us
    pallas_call x1, Pallas kernels: 40.8 us -> 39 us  [spectrum_call(): pl.pallas_call(functools.partial(spectrum_kernel, dims), out_shape=jax.Sh...]
where the time goes in v4:
time: 44.6 us; the launch traced here: 44.5 us
  Pallas kernels  43.8 us (98%)
  between operations  0.69 us (2%)
    pallas_call x1, Pallas kernels, spectrum_call(): pl.pallas_call(functools.partial(spectrum_kernel, dims), out_shape=jax.Sh...  39 us
    pallas_call x1, Pallas kernels, synthesis_call(): pl.pallas_call(synthesis_kernel, out_shape=(jax.ShapeDtypeStruct((rows, N...  4.77 us

profile of v4, /device:TPU:1, one launch (start us, length us, event | category | flops | bytes accessed | tf_op | source)
XLA Modules:
  0.0 44.5 jit_solution(14057547457679015224)
XLA Ops:
  0.6 0.0 copy-start
  0.6 0.0 copy-start.1
  0.7 0.0 copy-start.2
  0.7 39.0 %spectrum.1.spec_ref = f32[2,2,32,128]{3,2,1,0:T(8,128)S(1)} custom-call(s32[16,128]{1,0:T(8,128)} %bitcast.6, s32[32]{0:T(128)} %counts_hbm.1, f32[6,64]{1,0:T(8,128)} %bitcast.7, bf16[64,128,128]{2,1,0:T(8,128)(2,1)} %bitcast.5, bf16[64,2,2,6,16,128]{5,4,3,2,1,0:T(8,128)(2,1)} %sgt_hbm.1), custom_call_target="tpu_custom_call" | custom-call | tf_op jit(solution)/shard_map/spectrum/pallas_call | solution.py:410
  39.7 0.0 copy-done
  39.7 0.0 copy-done.1
  39.7 0.0 copy-done.2
  39.7 4.8 %synthesis.1 = (bf16[64,2048]{1,0:T(8,128)(2,1)}, f32[64,40]{1,0:T(8,128)}) custom-call(f32[2,2,32,128]{3,2,1,0:T(8,128)S(1)} %spectrum.1.spec_ref, f32[2,40,128]{2,1,0:T(8,128)S(1)} %copy-done.2, bf16[4,256,512]{2,1,0:T(8,128)(2,1)S(1)} %copy-done.1, bf16[4,256,512]{2,1,0:T(8,128)(2,1)S(1)} %copy-done), custom_call_target="tpu_custom_call" | custom-call | tf_op jit(solution)/shard_map/synthesis/pallas_call | solution.py:527
Async XLA Ops:
  0.6 39.1 %copy-start = (bf16[4,256,512]{2,1,0:T(8,128)(2,1)S(1)}, bf16[4,256,512]{2,1,0:T(8,128)(2,1)}, u32[]{:S(2)}) copy-start(bf16[4,256,512]{2,1,0:T(8,128)(2,1)} %constant.8.clone.low) | copy-start | bytes 3145732
  0.6 39.1 %copy-start.1 = (bf16[4,256,512]{2,1,0:T(8,128)(2,1)S(1)}, bf16[4,256,512]{2,1,0:T(8,128)(2,1)}, u32[]{:S(2)}) copy-start(bf16[4,256,512]{2,1,0:T(8,128)(2,1)} %constant.7.clone.high) | copy-start | bytes 3145732
  0.7 39.1 %copy-start.2 = (f32[2,40,128]{2,1,0:T(8,128)S(1)}, f32[2,40,128]{2,1,0:T(8,128)}, u32[]{:S(2)}) copy-start(f32[2,40,128]{2,1,0:T(8,128)} %constant.6.clone.gain_ref) | copy-start | bytes 122884
